TPU v7x, 32 devices: a whole 2x2x4 slice. The times are simulated.
32 devices in a mesh: req: 16 (over z, y, x), mlp: 2 (over core).
Axes of the slice: x: 2, y: 2, z: 4, core: 2. Of those that a mesh axis runs over, the one named last changes fastest.
Arguments:
- queries: bfloat16 [16, 256, 1536], P('req'), may hold values from -90 to 90
- cached_key_slots: bfloat16 [16, 8192, 512], P('req', 'mlp'), may hold values from -5 to 5
- cached_value_slots: bfloat16 [16, 8192, 512], P('req', 'mlp'), may hold values from -6 to 6
- new_token_keys: bfloat16 [16, 256, 512], P('req', 'mlp'), may hold values from -5.05 to 5.05
- new_token_values: bfloat16 [16, 256, 512], P('req', 'mlp'), may hold values from -6 to 6
- cache_len: int32 [16], replicated, may hold values from 1 to 8192, 65536 in all
- placing: int32 [16], replicated, may hold values from 0 to 15, each once
- w_gate: bfloat16 [1536, 12288], P('req', 'mlp'), may hold values from -0.15625 to 0.15625
- w_up: bfloat16 [1536, 12288], P('req', 'mlp'), may hold values from -0.15625 to 0.15625
- w_down: bfloat16 [12288, 1536], P('mlp', 'req'), may hold values from -0.0546875 to 0.0546875
Outputs:
- mixed: bfloat16 [16, 256, 1536], P('req', 'mlp')
All inputs are finite; a program needn't handle non-finite values.
Results may differ from a plain program's by a relative error of at most 0.019.
Values may be sent and summed in bfloat16 or wider, within the bound.
A program may use at most 192 MiB of HBM per device.

v0:
```python
import jax
import jax.numpy as jnp
from jax import lax
from jax.sharding import PartitionSpec as P

HEAD_SIZE = 256
QUERY_HEADS = 6
KEY_VALUE_HEADS = 2
score_scale = 0.0625
negative = -1e30


def lookup(table, index):
    positions = jnp.arange(table.shape[0], dtype=jnp.int32)
    return jnp.sum(jnp.where(positions == index, table, 0))


def rms_rows(attended):
    wide = attended.astype(jnp.float32)
    return (wide * lax.rsqrt(jnp.mean(wide * wide, axis=-1, keepdims=True) + 1e-06)).astype(
        jnp.bfloat16
    )


def gathered_weights(weighted, denom_local, w_gate, w_up, w_down):
    token_inputs = weighted.shape[0]
    mlp_index = lax.axis_index("mlp")
    row_count = token_inputs // lax.axis_size("mlp")
    weighted, denom = lax.psum((weighted, denom_local), "mlp")
    attended = (
        (weighted / jnp.transpose(denom, (2, 0, 1))[..., None])
        .reshape(token_inputs, QUERY_HEADS * HEAD_SIZE)
        .astype(jnp.bfloat16)
    )
    normed = rms_rows(attended)
    own_attended = lax.dynamic_slice_in_dim(attended, mlp_index * row_count, row_count, 0)
    gate_sum = jnp.dot(
        normed,
        lax.all_gather(w_gate, "req", axis=0, tiled=True),
        preferred_element_type=jnp.float32,
    )
    upper_sum = jnp.dot(
        normed, lax.all_gather(w_up, "req", axis=0, tiled=True), preferred_element_type=jnp.float32
    )
    hidden = (jax.nn.silu(gate_sum) * upper_sum).astype(jnp.bfloat16)
    partial_down = jnp.dot(
        hidden,
        lax.all_gather(w_down, "req", axis=1, tiled=True),
        preferred_element_type=jnp.float32,
    )
    own_rows = lax.psum_scatter(
        partial_down.astype(jnp.bfloat16), "mlp", scatter_dimension=0, tiled=True
    ).astype(jnp.float32)
    residual = own_attended.astype(jnp.float32)
    return (residual + own_rows).astype(jnp.bfloat16)[None]


def body(
    queries,
    cached_key_slots,
    cached_value_slots,
    new_token_keys,
    new_token_values,
    cache_len,
    placing,
    w_gate,
    w_up,
    w_down,
):
    slot_index = lax.axis_index("req")
    mlp_index = lax.axis_index("mlp")
    mlp_count = lax.axis_size("mlp")
    token_inputs = queries.shape[1]
    request_cache = cached_key_slots.shape[1]
    request_new_tokens = new_token_keys.shape[1]
    query_group_width = QUERY_HEADS // KEY_VALUE_HEADS
    row_count = token_inputs // mlp_count
    request = lookup(placing, slot_index)
    live_len = lookup(cache_len, request)
    query_head_rows = queries[0].reshape(
        token_inputs, KEY_VALUE_HEADS, query_group_width, HEAD_SIZE
    )
    request_keys = cached_key_slots[0].reshape(request_cache, KEY_VALUE_HEADS, HEAD_SIZE)
    request_values = cached_value_slots[0].reshape(request_cache, KEY_VALUE_HEADS, HEAD_SIZE)
    new_key_rows = new_token_keys[0].reshape(request_new_tokens, KEY_VALUE_HEADS, HEAD_SIZE)
    new_value_rows = new_token_values[0].reshape(request_new_tokens, KEY_VALUE_HEADS, HEAD_SIZE)
    cache_pos = mlp_index * request_cache + jnp.arange(request_cache, dtype=jnp.int32)
    cache_live = cache_pos < live_len
    scores_old = (
        jnp.einsum(
            "ngrd,cgd->grnc", query_head_rows, request_keys, preferred_element_type=jnp.float32
        )
        * score_scale
    )
    scores_old = jnp.where(cache_live[None, None, None, :], scores_old, negative)
    fresh_pos = mlp_index * request_new_tokens + jnp.arange(request_new_tokens, dtype=jnp.int32)
    causal = fresh_pos[None, :] <= jnp.arange(token_inputs, dtype=jnp.int32)[:, None]
    scores_new = (
        jnp.einsum(
            "ngrd,mgd->grnm", query_head_rows, new_key_rows, preferred_element_type=jnp.float32
        )
        * score_scale
    )
    scores_new = jnp.where(causal[None, None], scores_new, negative)
    local_top = jnp.maximum(scores_old.max(-1), scores_new.max(-1))
    row_top = lax.pmax(local_top, "mlp")
    expo_old = jnp.exp(scores_old - row_top[..., None])
    expo_new = jnp.exp(scores_new - row_top[..., None])
    denom_local = expo_old.sum(-1) + expo_new.sum(-1)
    probs_old = expo_old.astype(jnp.bfloat16)
    probs_new = expo_new.astype(jnp.bfloat16)
    weighted = jnp.einsum(
        "grnc,cgd->ngrd", probs_old, request_values, preferred_element_type=jnp.float32
    )
    weighted = weighted + jnp.einsum(
        "grnm,mgd->ngrd", probs_new, new_value_rows, preferred_element_type=jnp.float32
    )
    if lax.axis_size("req") > 16:
        return gathered_weights(weighted, denom_local, w_gate, w_up, w_down)
    w_in = jnp.stack([w_gate, w_up])
    w_in = lax.all_to_all(w_in, "req", split_axis=2, concat_axis=1, tiled=True)
    w_in = lax.all_gather(w_in, "mlp", axis=2, tiled=True)
    w_out = lax.all_to_all(w_down, "req", split_axis=0, concat_axis=1, tiled=True)
    w_out = lax.all_gather(w_out, "mlp", axis=0, tiled=True)
    denom_rows = jnp.transpose(denom_local, (2, 0, 1))
    weighted = lax.psum_scatter(weighted, "mlp", scatter_dimension=0, tiled=True)
    denom = lax.psum_scatter(denom_rows, "mlp", scatter_dimension=0, tiled=True)
    attended = (
        (weighted / denom[..., None])
        .reshape(row_count, QUERY_HEADS * HEAD_SIZE)
        .astype(jnp.bfloat16)
    )
    normed = lax.all_gather(rms_rows(attended), "req", axis=0, tiled=True)
    gate_sum = jnp.dot(normed, w_in[0], preferred_element_type=jnp.float32)
    upper_sum = jnp.dot(normed, w_in[1], preferred_element_type=jnp.float32)
    hidden = (jax.nn.silu(gate_sum) * upper_sum).astype(jnp.bfloat16)
    partial_down = jnp.dot(hidden, w_out, preferred_element_type=jnp.float32)
    own_rows = lax.psum_scatter(
        partial_down.astype(jnp.bfloat16), "req", scatter_dimension=0, tiled=True
    ).astype(jnp.float32)
    return (attended.astype(jnp.float32) + own_rows).astype(jnp.bfloat16)[None]


def solution(mesh):
    in_specs = (
        P("req", None, None),
        P("req", "mlp", None),
        P("req", "mlp", None),
        P("req", "mlp", None),
        P("req", "mlp", None),
        P(),
        P(),
        P("req", "mlp"),
        P("req", "mlp"),
        P("mlp", "req"),
    )
    out_specs = P("req", "mlp", None)
    return jax.shard_map(body, mesh=mesh, in_specs=in_specs, out_specs=out_specs, check_vma=False)
```

profile of v0, /device:TPU:0, one launch (start us, length us, event | category | flops | bytes accessed | tf_op | source)
XLA Modules:
  0.0 450.4 jit_solution(2439042109606651874)
XLA Ops:
  6.5 1.4 copy.59
  8.0 6.9 %reshape_squeeze.15 = bf16[4096,2,256]{2,1,0:T(2,128)(2,1)} reshape(bf16[1,4096,512]{2,1,0:T(8,128)(2,1)} %param.11) | data formatting | bytes 8388608 | tf_op jit(solution)/shard_map/reshape;squeeze | solution.py:83
  15.1 0.6 fusion.20
  15.8 1.3 fusion.21
  17.0 0.6 add_compare_fusion
  17.6 12.0 %bitcast_reduce_fusion = (f32[2,3,256]{2,1,0:T(4,128)S(1)}, f32[2,4096,256,3]{2,1,3,0:T(8,128)}) fusion(pred[4096]{0:T(1024)(128)(4,1)S(1)} %add_compare_fusion, bf16[256,2,3,256]{0,3,2,1:T(8,128)(2,1)S(1)} %bitcast.63, bf16[4096,2,256,1]{2,1,0,3:T(2,128)(2,1)} %bitcast.61), kind=kOutput, calls=%fused_computation.1 | convolution fusion | flops 3240098304 | bytes 30156800 | tf_op jit(solution)/shard_map/ngrd,cgd->grnc/dot_general | solution.py:90
  29.6 0.3 fusion.25
  29.9 2.6 pmax.7
  32.5 11.5 %fusion.1 = f32[2,3,256]{2,1,0:T(4,128)S(1)} fusion(f32[2,4096,256,3]{2,1,3,0:T(8,128)} %get-tuple-element.8, f32[2,3,256]{2,1,0:T(4,128)S(1)} %pmax.7, pred[4096]{0:T(1024)(128)(4,1)S(1)} %add_compare_fusion), kind=kLoop, calls=%fused_computation.4 | loop fusion | flops 25164288 | bytes 25182208 | tf_op jit(solution)/shard_map/reduce_sum | solution.py:109
  44.0 0.1 fusion.12
  44.2 0.8 copy.94
  45.0 1.5 pad_maximum_fusion
  46.5 5.3 %copy.69 = bf16[2,96,6144]{1,0,2:T(2,128)(2,1)} copy(bf16[2,96,6144]{2,1,0:T(8,128)(2,1)S(1)} %pad_maximum_fusion) | data formatting | bytes 4718592 | tf_op jit(solution)/shard_map/stack | solution.py:120
  51.9 8.2 %all-to-all-start = ((bf16[2,96,6144]{1,0,2:T(2,128)(2,1)}), bf16[2,96,6144]{1,0,2:T(2,128)(2,1)S(1)}, u32[]{:S(2)}, u32[]{:S(2)}) async-start(bf16[2,96,6144]{1,0,2:T(2,128)(2,1)} %copy.69), calls=%async_computation.1 | async-start | bytes 6291456 | tf_op jit(solution)/shard_map/all_to_all | solution.py:121
  60.1 6.9 %reshape_squeeze.18 = bf16[4096,2,256]{2,1,0:T(2,128)(2,1)} reshape(bf16[1,4096,512]{2,1,0:T(8,128)(2,1)} %param.12) | data formatting | bytes 8388608 | tf_op jit(solution)/shard_map/reshape;squeeze | solution.py:84
  67.1 13.5 %fusion.3 = f32[2,3,256,256]{3,2,1,0:T(8,128)S(1)} fusion(f32[2,4096,256,3]{2,1,3,0:T(8,128)} %get-tuple-element.8, f32[2,3,256]{2,1,0:T(4,128)S(1)} %pmax.7, pred[4096]{0:T(1024)(128)(4,1)S(1)} %add_compare_fusion, bf16[4096,2,256,1]{2,1,0,3:T(2,128)(2,1)} %bitcast.62), kind=kOutput, calls=%fused_computation.6 | convolution fusion | flops 3246391296 | bytes 30943232 | tf_op jit(solution)/shard_map/grnc,cgd->ngrd/dot_general | solution.py:112
  80.6 1.6 add_bitcast_fusion
  82.3 38.9 %all-to-all-done = bf16[2,96,6144]{1,0,2:T(2,128)(2,1)S(1)} async-done(((bf16[2,96,6144]{1,0,2:T(2,128)(2,1)}), bf16[2,96,6144]{1,0,2:T(2,128)(2,1)S(1)}, u32[]{:S(2)}, u32[]{:S(2)}) %all-to-all-start) | async-done | bytes 2359328 | tf_op jit(solution)/shard_map/all_to_all | solution.py:121
  121.2 5.5 %copy.91 = bf16[2,96,16,384]{3,1,2,0:T(8,128)(2,1)} copy(bf16[2,96,16,384]{1,0,3,2:T(2,128)(2,1)S(1)} %bitcast.56) | data formatting | bytes 4718592 | tf_op jit(solution)/shard_map/all_to_all | solution.py:121
  126.8 1.0 reshape.52
  128.0 1.4 multiply_reduce_fusion
  129.4 0.3 copy.68
  129.7 0.8 multiply_convert_fusion.1
  130.7 44.9 %all_to_all.37 = bf16[16,384,96]{1,2,0:T(8,128)(2,1)} all-to-all(bf16[16,384,96]{1,2,0:T(8,128)(2,1)S(1)} %bitcast.60), channel_id=1, replica_groups=mesh['req'=16,'mlp'=2] {'req'}, dimensions={0} | all-to-all | bytes 2359296 | tf_op jit(solution)/shard_map/all_to_all | solution.py:123
  175.6 0.2 reduce-scatter.8.cloned.1.call-start
  175.9 96.7 %all-gather.4.cloned.1.call-done = bf16[2048,1536]{0,1:T(8,128)(2,1)} async-done(((bf16[128,1536]{0,1:T(8,128)(2,1)}), bf16[2048,1536]{0,1:T(8,128)(2,1)}) %all-gather.4.cloned.1.call-update) | async-done | bytes 6291472 | tf_op jit(solution)/shard_map/all_gather | solution.py:133
  272.6 8.3 %fusion.9 = f32[2048,768]{1,0:T(8,128)S(1)} fusion(bf16[2048,1536]{0,1:T(8,128)(2,1)} %all-gather.4.cloned.1.call-done, bf16[2,1536,768]{2,1,0:T(8,128)(2,1)} %all-gather.6.cloned.1.call-done), kind=kOutput, calls=%fused_computation.15 | convolution fusion | flops 4831838208 | bytes 14942208 | tf_op jit(solution)/shard_map/dot_general | solution.py:134
  280.9 7.6 %multiply_convert_fusion = bf16[2048,768]{1,0:T(8,128)(2,1)} fusion(f32[2048,768]{1,0:T(8,128)S(1)} %fusion.9, bf16[2048,1536]{0,1:T(8,128)(2,1)S(1)} %copy-done.6, bf16[2,1536,768]{2,1,0:T(8,128)(2,1)S(1)} %copy-done.7), kind=kOutput, calls=%fused_computation.9 | convolution fusion | flops 4841275392 | bytes 18087936 | tf_op jit(solution)/shard_map/dot_general | solution.py:135
  288.5 9.1 %convolution_convert_fusion = bf16[2048,1536]{1,0:T(8,128)(2,1)} fusion(bf16[2048,768]{1,0:T(8,128)(2,1)} %multiply_convert_fusion, bf16[768,1536]{0,1:T(8,128)(2,1)} %all-gather.8.cloned.1.call-done), kind=kOutput, calls=%fused_computation.8 | convolution fusion | flops 4834983936 | bytes 11796480 | tf_op jit(solution)/shard_map/dot_general | solution.py:137
  297.7 0.3 copy.73
  298.0 143.7 %reduce-scatter.8.cloned.1.call-done = bf16[128,1536]{1,0:T(8,128)(2,1)} async-done(((bf16[2048,1536]{1,0:T(8,128)(2,1)}), bf16[128,1536]{1,0:T(8,128)(2,1)}) %reduce-scatter.8.cloned.1.call-update) | async-done | bytes 393232 | tf_op jit(solution)/shard_map/reduce_scatter | solution.py:138
  441.7 1.8 fusion.16
  (45 shorter events, 0.7 us)
Async XLA Ops:
  6.5 120.3 %reduce-scatter.10.cloned.1.call-start = ((), (), s32[]{:S(2)}) async-start(), calls=%async_computation.10 | async-start | bytes 196608
  6.5 8.4 %copy-start.4 = (bf16[1,128,512]{2,1,0:T(8,128)(2,1)S(1)}, bf16[1,128,512]{2,1,0:T(8,128)(2,1)}, u32[]{:S(2)}) copy-start(bf16[1,128,512]{2,1,0:T(8,128)(2,1)} %param.13) | copy-start | bytes 393220
  8.0 7.1 %copy-start.8 = (s32[16]{0:T(128)S(1)}, s32[16]{0:T(128)}, u32[]{:S(2)}) copy-start(s32[16]{0:T(128)} %param.16) | copy-start | bytes 196
  8.0 7.8 %copy-start.9 = (s32[16]{0:T(128)S(1)}, s32[16]{0:T(128)}, u32[]{:S(2)}) copy-start(s32[16]{0:T(128)} %param.15) | copy-start | bytes 196
  29.8 14.2 %copy-start = (f32[2,3,256,128]{2,3,1,0:T(8,128)}, f32[2,3,256,128]{2,3,1,0:T(8,128)S(1)}, u32[]{:S(2)}) copy-start(f32[2,3,256,128]{2,3,1,0:T(8,128)S(1)} %get-tuple-element.10) | copy-start | bytes 2359300
  32.5 12.5 %copy-start.3 = (bf16[96,6144]{1,0:T(8,128)(2,1)S(1)}, bf16[96,6144]{1,0:T(8,128)(2,1)}, u32[]{:S(2)}) copy-start(bf16[96,6144]{1,0:T(8,128)(2,1)} %param.18) | copy-start | bytes 3538948
  51.9 69.4 %all-to-all-start = ((bf16[2,96,6144]{1,0,2:T(2,128)(2,1)}), bf16[2,96,6144]{1,0,2:T(2,128)(2,1)S(1)}, u32[]{:S(2)}, u32[]{:S(2)}) async-start(bf16[2,96,6144]{1,0,2:T(2,128)(2,1)} %copy.69), calls=%async_computation.1 | async-start | bytes 6291456 | tf_op jit(solution)/shard_map/all_to_all | solution.py:121
  60.1 7.0 %copy-start.5 = (bf16[1,128,512]{2,1,0:T(8,128)(2,1)S(1)}, bf16[1,128,512]{2,1,0:T(8,128)(2,1)}, u32[]{:S(2)}) copy-start(bf16[1,128,512]{2,1,0:T(8,128)(2,1)} %param.14) | copy-start | bytes 393220
  60.1 67.9 %reduce-scatter.6.cloned.1.call-start = ((), (), s32[]{:S(2)}) async-start(), calls=%async_computation.5 | async-start | bytes 2359296 | tf_op jit(solution)/shard_map/reduce_scatter | solution.py:126
  67.1 13.5 %copy-start.1 = (f32[2,3,256,128]{2,3,1,0:T(8,128)S(1)}, f32[2,3,256,128]{2,3,1,0:T(8,128)}, u32[]{:S(2)}) copy-start(f32[2,3,256,128]{2,3,1,0:T(8,128)} %copy-done) | copy-start | bytes 2359300
  82.3 93.6 %all-gather.6.cloned.1.call-start = ((), (), s32[]{:S(2)}) async-start(), calls=%async_computation.7 | async-start | bytes 7077888 | tf_op jit(solution)/shard_map/all_gather | solution.py:122
  126.7 3.8 copy-start.2
  126.8 145.9 %all-gather.4.cloned.1.call-start = ((), (), s32[]{:S(2)}) async-start(), calls=%async_computation.6 | async-start | bytes 6684672 | tf_op jit(solution)/shard_map/all_gather | solution.py:133
  130.5 158.1 %all-gather.8.cloned.1.call-start = ((), (), s32[]{:S(2)}) async-start(), calls=%async_computation.8 | async-start | bytes 3538944 | tf_op jit(solution)/shard_map/all_gather | solution.py:124
  175.6 266.1 %reduce-scatter.8.cloned.1.call-start = ((), (), s32[]{:S(2)}) async-start(), calls=%async_computation.9 | async-start | bytes 6684672 | tf_op jit(solution)/shard_map/reduce_scatter | solution.py:138
  272.6 8.3 %copy-start.6 = (bf16[2048,1536]{0,1:T(8,128)(2,1)S(1)}, bf16[2048,1536]{0,1:T(8,128)(2,1)}, u32[]{:S(2)}) copy-start(bf16[2048,1536]{0,1:T(8,128)(2,1)} %all-gather.4.cloned.1.call-done) | copy-start | bytes 18874372
  272.6 8.3 %copy-start.7 = (bf16[2,1536,768]{2,1,0:T(8,128)(2,1)S(1)}, bf16[2,1536,768]{2,1,0:T(8,128)(2,1)}, u32[]{:S(2)}) copy-start(bf16[2,1536,768]{2,1,0:T(8,128)(2,1)} %all-gather.6.cloned.1.call-done) | copy-start | bytes 14155780
Sparse Core Ops, SparseCore 0:
  45.1 10.0 reduce-scatter.9
  82.4 10.3 reduce-scatter.5
  126.9 24.3 all-gather.5
  154.2 118.3 all-gather.3
  274.1 9.0 all-gather.7
  297.8 143.8 reduce-scatter.7
where the time goes:
time: 451 us; the launch traced here: 450 us
  waiting for transfers between devices  280 us (62%)
  matrix products  52.4 us (12%)
  blocking collectives  47.6 us (11%)
  local copies, waits for them, and re-layouts  28.9 us (6%)
  other arithmetic  19.7 us (4%)
  between operations  13.7 us (3%)
  starting transfers between devices  8.58 us (2%)
    reduce_scatter x1, waiting for transfers between devices, body(): lax.psum_scatter(partial_down.astype(jnp.bfloat16), 'req', scatter_dimens...  144 us
    all_gather x1, waiting for transfers between devices, body(): normed = lax.all_gather(rms_rows(attended), 'req', axis=0, tiled=True)  96.7 us
    all_to_all x1, blocking collectives, body(): lax.all_to_all(w_down, 'req', split_axis=0, concat_axis=1, tiled=True)  44.9 us
    all_to_all x1, waiting for transfers between devices, body(): w_in = lax.all_to_all(w_in, 'req', split_axis=2, concat_axis=1, tiled=True)  38.9 us
    dot_general x1, matrix products, body(): jnp.einsum('grnc,cgd->ngrd', probs_old, request_values, preferred_element...  13.5 us
    dot_general x1, matrix products, body(): jnp.einsum('ngrd,cgd->grnc', query_head_rows, request_keys, preferred_ele...  12 us
    reduce_sum x2, other arithmetic, body(): denom_local = expo_old.sum(-1) + expo_new.sum(-1)  11.7 us
    dot_general x1, matrix products, body(): partial_down = jnp.dot(hidden, w_out, preferred_element_type=jnp.float32)  9.13 us
  transfers between devices with their start and end apart: 7, of which 3 were waited for; matrix products, arithmetic and copies ran while one was open for 12% of the time, Pallas kernels for 0%

commit v1 on v0

--- a/solution.py
+++ b/solution.py
@@ -8,6 +8,12 @@
 KEY_VALUE_HEADS = 2
 score_scale = 0.0625
 negative = -1e30
+
+
+def joined_along(tiles, dim):
+    lengths = list(tiles.shape[1:])
+    lengths[dim] *= tiles.shape[0]
+    return jnp.moveaxis(tiles, 0, dim).reshape(lengths)
 
 
 def lookup(table, index):
@@ -130,7 +136,20 @@
         .reshape(row_count, QUERY_HEADS * HEAD_SIZE)
         .astype(jnp.bfloat16)
     )
-    normed = lax.all_gather(rms_rows(attended), "req", axis=0, tiled=True)
+    array = rms_rows(attended)
+    length = lax.axis_size("req")
+    pairs = [(i, (i + 1) % length) for i in range(length)]
+    back = [(b, a) for a, b in pairs]
+    lower, upper = ([], [])
+    for step in range(length - 1):
+        if step % 2 == 0:
+            lower.append(lax.ppermute(lower[-1] if lower else array, "req", pairs))
+        else:
+            upper.append(lax.ppermute(upper[-1] if upper else array, "req", back))
+    blocks = jnp.stack([*lower[::-1], array, *upper])
+    shift = lax.axis_index("req") - len(lower)
+    blocks = blocks[(jnp.arange(length) - shift) % length]
+    normed = joined_along(blocks, 0)
     gate_sum = jnp.dot(normed, w_in[0], preferred_element_type=jnp.float32)
     upper_sum = jnp.dot(normed, w_in[1], preferred_element_type=jnp.float32)
     hidden = (jax.nn.silu(gate_sum) * upper_sum).astype(jnp.bfloat16)

time: 451 us -> 505 us (1.12)
  starting transfers between devices: 8.58 us -> 80.5 us
  blocking collectives: 47.6 us -> 2.62 us
  local copies, waits for them, and re-layouts: 28.9 us -> 67.6 us
  waiting for transfers between devices: 280 us -> 267 us
    all_gather x1 -> x0, waiting for transfers between devices: 96.7 us -> none  [body(): normed = lax.all_gather(rms_rows(attended), 'req', axis=0, tiled=True)]
    ppermute x0 -> x15, waiting for transfers between devices: none -> 79.2 us  [the longest x7 47.9 us: body(): upper.append(lax.ppermute(upper[-1] if upper else array, 'req', back))]
    ppermute x0 -> x15, starting transfers between devices: none -> 67.5 us  [the longest x7 61.8 us: body(): upper.append(lax.ppermute(upper[-1] if upper else array, 'req', back))]
    all_to_all x1 -> x0, blocking collectives: 44.9 us -> none  [body(): lax.all_to_all(w_down, 'req', split_axis=0, concat_axis=1, tiled=True)]
    unnamed x25 -> x51, local copies, waits for them, and re-layouts: 3.42 us -> 25.1 us
    gather x0 -> x2, local copies, waits for them, and re-layouts: none -> 15.4 us  [body(): blocks = blocks[(jnp.arange(length) - shift) % length]]
    reduce_scatter x1, waiting for transfers between devices: 144 us -> 149 us  [body(): lax.psum_scatter(partial_down.astype(jnp.bfloat16), 'req', scatter_dimens...]
  transfers between devices with their start and end apart: 7 -> 22, of which waited for: 3 -> 10; matrix products, arithmetic and copies ran while one was open for 12% -> 18% of each run, Pallas kernels for 0% -> 0%
where the time goes in v1:
time: 505 us; the launch traced here: 504 us
  waiting for transfers between devices  267 us (53%)
  starting transfers between devices  80.5 us (16%)
  local copies, waits for them, and re-layouts  67.6 us (13%)
  matrix products  51.4 us (10%)
  other arithmetic  20.6 us (4%)
  between operations  13.4 us (3%)
    reduce_scatter x1, waiting for transfers between devices, body(): lax.psum_scatter(partial_down.astype(jnp.bfloat16), 'req', scatter_dimens...  149 us
    ppermute x7, starting transfers between devices, body(): upper.append(lax.ppermute(upper[-1] if upper else array, 'req', back))  61.8 us
    ppermute x7, waiting for transfers between devices, body(): upper.append(lax.ppermute(upper[-1] if upper else array, 'req', back))  47.9 us
    all_to_all x1, waiting for transfers between devices, body(): w_in = lax.all_to_all(w_in, 'req', split_axis=2, concat_axis=1, tiled=True)  39 us
    ppermute x8, waiting for transfers between devices, body(): lower.append(lax.ppermute(lower[-1] if lower else array, 'req', pairs))  31.3 us
    unnamed x51, local copies, waits for them, and re-layouts  25.1 us
    gather x2, local copies, waits for them, and re-layouts, body(): blocks = blocks[(jnp.arange(length) - shift) % length]  15.4 us
    dot_general x1, matrix products, body(): jnp.einsum('grnc,cgd->ngrd', probs_old, request_values, preferred_element...  13.5 us
  transfers between devices with their start and end apart: 22, of which 10 were waited for; matrix products, arithmetic and copies ran while one was open for 18% of the time, Pallas kernels for 0%

profile of v1, /device:TPU:0, one launch (start us, length us, event | category | flops | bytes accessed | tf_op | source)
XLA Modules:
  0.0 503.5 jit_solution(8349686826563594058)
XLA Ops:
  8.0 6.9 %reshape_squeeze.15 = bf16[4096,2,256]{2,1,0:T(2,128)(2,1)} reshape(bf16[1,4096,512]{2,1,0:T(8,128)(2,1)} %param.11) | data formatting | bytes 8388608 | tf_op jit(solution)/shard_map/reshape;squeeze | solution.py:89
  17.5 12.0 %bitcast_reduce_fusion = (f32[2,3,256]{2,1,0:T(4,128)S(1)}, f32[2,4096,256,3]{2,1,3,0:T(8,128)}) fusion(pred[4096]{0:T(1024)(128)(4,1)S(1)} %add_compare_fusion, bf16[256,2,3,256]{0,3,2,1:T(8,128)(2,1)S(1)} %bitcast.99, bf16[4096,2,256,1]{2,1,0,3:T(2,128)(2,1)} %bitcast.97), kind=kOutput, calls=%fused_computation.2 | convolution fusion | flops 3240098304 | bytes 30156800 | tf_op jit(solution)/shard_map/ngrd,cgd->grnc/dot_general | solution.py:96
  29.8 2.6 pmax.7
  32.5 11.5 %fusion.1 = f32[2,3,256]{2,1,0:T(4,128)S(1)} fusion(f32[2,4096,256,3]{2,1,3,0:T(8,128)} %get-tuple-element.8, f32[2,3,256]{2,1,0:T(4,128)S(1)} %pmax.7, pred[4096]{0:T(1024)(128)(4,1)S(1)} %add_compare_fusion), kind=kLoop, calls=%fused_computation.5 | loop fusion | flops 25164288 | bytes 25182208 | tf_op jit(solution)/shard_map/reduce_sum | solution.py:115
  46.5 5.3 %copy.76 = bf16[2,96,6144]{1,0,2:T(2,128)(2,1)} copy(bf16[2,96,6144]{2,1,0:T(8,128)(2,1)S(1)} %pad_maximum_fusion) | data formatting | bytes 4718592 | tf_op jit(solution)/shard_map/stack | solution.py:126
  51.8 8.3 %all-to-all-start = ((bf16[2,96,6144]{1,0,2:T(2,128)(2,1)}), bf16[2,96,6144]{1,0,2:T(2,128)(2,1)S(1)}, u32[]{:S(2)}, u32[]{:S(2)}) async-start(bf16[2,96,6144]{1,0,2:T(2,128)(2,1)} %copy.76), calls=%async_computation.1 | async-start | bytes 6291456 | tf_op jit(solution)/shard_map/all_to_all | solution.py:127
  60.2 6.9 %reshape_squeeze.18 = bf16[4096,2,256]{2,1,0:T(2,128)(2,1)} reshape(bf16[1,4096,512]{2,1,0:T(8,128)(2,1)} %param.12) | data formatting | bytes 8388608 | tf_op jit(solution)/shard_map/reshape;squeeze | solution.py:90
  67.2 13.5 %fusion.3 = f32[2,3,256,256]{3,2,1,0:T(8,128)S(1)} fusion(f32[2,4096,256,3]{2,1,3,0:T(8,128)} %get-tuple-element.8, f32[2,3,256]{2,1,0:T(4,128)S(1)} %pmax.7, pred[4096]{0:T(1024)(128)(4,1)S(1)} %add_compare_fusion, bf16[4096,2,256,1]{2,1,0,3:T(2,128)(2,1)} %bitcast.98), kind=kOutput, calls=%fused_computation.7 | convolution fusion | flops 3246391296 | bytes 30943232 | tf_op jit(solution)/shard_map/grnc,cgd->ngrd/dot_general | solution.py:118
  82.3 39.0 %all-to-all-done = bf16[2,96,6144]{1,0,2:T(2,128)(2,1)S(1)} async-done(((bf16[2,96,6144]{1,0,2:T(2,128)(2,1)}), bf16[2,96,6144]{1,0,2:T(2,128)(2,1)S(1)}, u32[]{:S(2)}, u32[]{:S(2)}) %all-to-all-start) | async-done | bytes 2359328 | tf_op jit(solution)/shard_map/all_to_all | solution.py:127
  121.3 5.4 %copy.98 = bf16[2,96,16,384]{3,1,2,0:T(8,128)(2,1)} copy(bf16[2,96,16,384]{1,0,3,2:T(2,128)(2,1)S(1)} %bitcast.92) | data formatting | bytes 4718592 | tf_op jit(solution)/shard_map/all_to_all | solution.py:127
  130.4 2.7 collective-permute-start
  133.1 19.8 %collective-permute-done = bf16[128,1536]{0,1:T(8,128)(2,1)S(1)} collective-permute-done((bf16[128,1536]{0,1:T(8,128)(2,1)}, bf16[128,1536]{0,1:T(8,128)(2,1)S(1)}, u32[]{:S(2)}, u32[]{:S(2)}) %collective-permute-start) | collective-permute-done | bytes 393248 | tf_op jit(solution)/shard_map/ppermute | solution.py:146
  152.9 5.6 %collective-permute-start.8 = (bf16[128,1536]{0,1:T(8,128)(2,1)}, bf16[128,1536]{0,1:T(8,128)(2,1)S(1)}, u32[]{:S(2)}, u32[]{:S(2)}) collective-permute-start(bf16[128,1536]{0,1:T(8,128)(2,1)} %multiply_convert_fusion.2), channel_id=1, source_target_pairs={{2,0},{4,2},{6,4},{8,6},{10,8},{12,10},{14,12},{16,14},{18,16},{20... | collective-permute-start | bytes 1179656 | tf_op jit(solution)/shard_map/ppermute | solution.py:148
  158.5 10.0 %collective-permute-done.1 = bf16[128,1536]{0,1:T(8,128)(2,1)} collective-permute-done((bf16[128,1536]{0,1:T(8,128)(2,1)S(1)}, bf16[128,1536]{0,1:T(8,128)(2,1)}, u32[]{:S(2)}, u32[]{:S(2)}) %collective-permute-start.1) | collective-permute-done | bytes 393248 | tf_op jit(solution)/shard_map/ppermute | solution.py:146
  172.3 4.4 all-to-all-start.1
  176.8 5.8 %collective-permute-start.9 = (bf16[128,1536]{0,1:T(8,128)(2,1)S(1)}, bf16[128,1536]{0,1:T(8,128)(2,1)S(1)}, u32[]{:S(2)}, u32[]{:S(2)}) collective-permute-start(bf16[128,1536]{0,1:T(8,128)(2,1)S(1)} %collective-permute-done.8), channel_id=1, source_target_pairs={{2,0},{4,2},{6,4},{8,6},{10,8},{12,10},{14,12},{16,14},{18,16},{20... | collective-permute-start | bytes 1179656 | tf_op jit(solution)/shard_map/ppermute | solution.py:148
  184.1 19.0 %collective-permute-done.9 = bf16[128,1536]{0,1:T(8,128)(2,1)S(1)} collective-permute-done((bf16[128,1536]{0,1:T(8,128)(2,1)S(1)}, bf16[128,1536]{0,1:T(8,128)(2,1)S(1)}, u32[]{:S(2)}, u32[]{:S(2)}) %collective-permute-start.9) | collective-permute-done | bytes 393248 | tf_op jit(solution)/shard_map/ppermute | solution.py:148
  203.1 7.1 %collective-permute-start.10 = (bf16[128,1536]{0,1:T(8,128)(2,1)S(1)}, bf16[128,1536]{0,1:T(8,128)(2,1)S(1)}, u32[]{:S(2)}, u32[]{:S(2)}) collective-permute-start(bf16[128,1536]{0,1:T(8,128)(2,1)S(1)} %collective-permute-done.9), channel_id=1, source_target_pairs={{2,0},{4,2},{6,4},{8,6},{10,8},{12,10},{14,12},{16,14},{18,16},{20... | collective-permute-start | bytes 1179656 | tf_op jit(solution)/shard_map/ppermute | solution.py:148
  210.2 7.2 %collective-permute-done.10 = bf16[128,1536]{0,1:T(8,128)(2,1)S(1)} collective-permute-done((bf16[128,1536]{0,1:T(8,128)(2,1)S(1)}, bf16[128,1536]{0,1:T(8,128)(2,1)S(1)}, u32[]{:S(2)}, u32[]{:S(2)}) %collective-permute-start.10) | collective-permute-done | bytes 393248 | tf_op jit(solution)/shard_map/ppermute | solution.py:148
  217.3 10.5 %collective-permute-start.11 = (bf16[128,1536]{0,1:T(8,128)(2,1)S(1)}, bf16[128,1536]{0,1:T(8,128)(2,1)S(1)}, u32[]{:S(2)}, u32[]{:S(2)}) collective-permute-start(bf16[128,1536]{0,1:T(8,128)(2,1)S(1)} %collective-permute-done.10), channel_id=1, source_target_pairs={{2,0},{4,2},{6,4},{8,6},{10,8},{12,10},{14,12},{16,14},{18,16},{20... | collective-permute-start | bytes 1179656 | tf_op jit(solution)/shard_map/ppermute | solution.py:148
  228.2 8.2 %collective-permute-done.11 = bf16[128,1536]{0,1:T(8,128)(2,1)S(1)} collective-permute-done((bf16[128,1536]{0,1:T(8,128)(2,1)S(1)}, bf16[128,1536]{0,1:T(8,128)(2,1)S(1)}, u32[]{:S(2)}, u32[]{:S(2)}) %collective-permute-start.11) | collective-permute-done | bytes 393248 | tf_op jit(solution)/shard_map/ppermute | solution.py:148
  237.1 10.9 %collective-permute-start.12 = (bf16[128,1536]{0,1:T(8,128)(2,1)S(1)}, bf16[128,1536]{0,1:T(8,128)(2,1)}, u32[]{:S(2)}, u32[]{:S(2)}) collective-permute-start(bf16[128,1536]{0,1:T(8,128)(2,1)S(1)} %collective-permute-done.11), channel_id=1, source_target_pairs={{2,0},{4,2},{6,4},{8,6},{10,8},{12,10},{14,12},{16,14},{18,16},{20... | collective-permute-start | bytes 1179656 | tf_op jit(solution)/shard_map/ppermute | solution.py:148
  248.0 7.7 %collective-permute-done.12 = bf16[128,1536]{0,1:T(8,128)(2,1)} collective-permute-done((bf16[128,1536]{0,1:T(8,128)(2,1)S(1)}, bf16[128,1536]{0,1:T(8,128)(2,1)}, u32[]{:S(2)}, u32[]{:S(2)}) %collective-permute-start.12) | collective-permute-done | bytes 393248 | tf_op jit(solution)/shard_map/ppermute | solution.py:148
  255.7 10.9 %collective-permute-start.13 = (bf16[128,1536]{0,1:T(8,128)(2,1)}, bf16[128,1536]{0,1:T(8,128)(2,1)}, u32[]{:S(2)}, u32[]{:S(2)}) collective-permute-start(bf16[128,1536]{0,1:T(8,128)(2,1)} %collective-permute-done.12), channel_id=1, source_target_pairs={{2,0},{4,2},{6,4},{8,6},{10,8},{12,10},{14,12},{16,14},{18,16},{20... | collective-permute-start | bytes 1179656 | tf_op jit(solution)/shard_map/ppermute | solution.py:148
  267.9 5.8 %collective-permute-done.13 = bf16[128,1536]{0,1:T(8,128)(2,1)} collective-permute-done((bf16[128,1536]{0,1:T(8,128)(2,1)}, bf16[128,1536]{0,1:T(8,128)(2,1)}, u32[]{:S(2)}, u32[]{:S(2)}) %collective-permute-start.13) | collective-permute-done | bytes 393248 | tf_op jit(solution)/shard_map/ppermute | solution.py:148
  273.8 11.0 %collective-permute-start.14 = (bf16[128,1536]{0,1:T(8,128)(2,1)}, bf16[128,1536]{0,1:T(8,128)(2,1)S(1)}, u32[]{:S(2)}, u32[]{:S(2)}) collective-permute-start(bf16[128,1536]{0,1:T(8,128)(2,1)} %collective-permute-done.13), channel_id=1, source_target_pairs={{2,0},{4,2},{6,4},{8,6},{10,8},{12,10},{14,12},{16,14},{18,16},{20... | collective-permute-start | bytes 1179656 | tf_op jit(solution)/shard_map/ppermute | solution.py:148
  306.3 6.8 %gather_fusion = bf16[16,128,1536]{1,2,0:T(8,128)(2,1)} fusion(bf16[16,128,1536]{1,2,0:T(8,128)(2,1)} %bitcast_dynamic-update-slice_fusion, s32[1024]{0:T(1024)S(1)} %pad_clamp_fusion), kind=kCustom, calls=%fused_computation | custom fusion | bytes 12582976 | tf_op jit(solution)/shard_map/gather | solution.py:151
  313.0 8.6 %copy.75 = bf16[16,128,1536]{2,1,0:T(8,128)(2,1)} copy(bf16[16,128,1536]{1,2,0:T(8,128)(2,1)} %gather_fusion) | data formatting | bytes 12582912 | tf_op jit(solution)/shard_map/gather | solution.py:151
  321.7 8.0 %fusion.9 = f32[2048,768]{1,0:T(8,128)S(1)} fusion(bf16[2048,1536]{1,0:T(8,128)(2,1)} %bitcast.94, bf16[2,1536,768]{2,1,0:T(8,128)(2,1)} %all-gather.3.cloned.1.call-done), kind=kOutput, calls=%fused_computation.16 | convolution fusion | flops 4831838208 | bytes 14942208 | tf_op jit(solution)/shard_map/dot_general | solution.py:153
  329.7 6.9 %multiply_convert_fusion = bf16[2048,768]{1,0:T(8,128)(2,1)} fusion(f32[2048,768]{1,0:T(8,128)S(1)} %fusion.9, bf16[2048,1536]{1,0:T(8,128)(2,1)S(1)} %bitcast.95, bf16[2,1536,768]{2,1,0:T(8,128)(2,1)S(1)} %copy-done.13), kind=kOutput, calls=%fused_computation.10 | convolution fusion | flops 4841275392 | bytes 18087936 | tf_op jit(solution)/shard_map/dot_general | solution.py:154
  336.6 9.1 %convolution_convert_fusion = bf16[2048,1536]{1,0:T(8,128)(2,1)} fusion(bf16[2048,768]{1,0:T(8,128)(2,1)} %multiply_convert_fusion, bf16[768,1536]{0,1:T(8,128)(2,1)} %all-gather.5.cloned.1.call-done), kind=kOutput, calls=%fused_computation.9 | convolution fusion | flops 4834983936 | bytes 11796480 | tf_op jit(solution)/shard_map/dot_general | solution.py:156
  346.1 149.1 %reduce-scatter.8.cloned.1.call-done = bf16[128,1536]{1,0:T(8,128)(2,1)} async-done(((bf16[2048,1536]{1,0:T(8,128)(2,1)}), bf16[128,1536]{1,0:T(8,128)(2,1)}) %reduce-scatter.8.cloned.1.call-update) | async-done | bytes 393232 | tf_op jit(solution)/shard_map/reduce_scatter | solution.py:157
  (105 shorter events, 43.5 us)
Async XLA Ops:
  6.5 9.2 %copy-start.15 = (s32[16]{0:T(128)S(1)}, s32[16]{0:T(128)}, u32[]{:S(2)}) copy-start(s32[16]{0:T(128)} %param.15) | copy-start | bytes 196
  6.5 120.3 %reduce-scatter.10.cloned.1.call-start = ((), (), s32[]{:S(2)}) async-start(), calls=%async_computation.9 | async-start | bytes 196608
  29.8 14.2 %copy-start = (f32[2,3,256,128]{2,3,1,0:T(8,128)}, f32[2,3,256,128]{2,3,1,0:T(8,128)S(1)}, u32[]{:S(2)}) copy-start(f32[2,3,256,128]{2,3,1,0:T(8,128)S(1)} %get-tuple-element.10) | copy-start | bytes 2359300
  32.5 12.5 %copy-start.5 = (bf16[96,6144]{1,0:T(8,128)(2,1)S(1)}, bf16[96,6144]{1,0:T(8,128)(2,1)}, u32[]{:S(2)}) copy-start(bf16[96,6144]{1,0:T(8,128)(2,1)} %param.18) | copy-start | bytes 3538948
  51.8 15.3 %copy-start.12 = (bf16[1,128,512]{2,1,0:T(8,128)(2,1)S(1)}, bf16[1,128,512]{2,1,0:T(8,128)(2,1)}, u32[]{:S(2)}) copy-start(bf16[1,128,512]{2,1,0:T(8,128)(2,1)} %param.14) | copy-start | bytes 393220
  51.8 69.5 %all-to-all-start = ((bf16[2,96,6144]{1,0,2:T(2,128)(2,1)}), bf16[2,96,6144]{1,0,2:T(2,128)(2,1)S(1)}, u32[]{:S(2)}, u32[]{:S(2)}) async-start(bf16[2,96,6144]{1,0,2:T(2,128)(2,1)} %copy.76), calls=%async_computation.1 | async-start | bytes 6291456 | tf_op jit(solution)/shard_map/all_to_all | solution.py:127
  60.1 67.8 %reduce-scatter.6.cloned.1.call-start = ((), (), s32[]{:S(2)}) async-start(), calls=%async_computation.5 | async-start | bytes 2359296 | tf_op jit(solution)/shard_map/reduce_scatter | solution.py:132
  67.1 13.5 %copy-start.1 = (f32[2,3,256,128]{2,3,1,0:T(8,128)S(1)}, f32[2,3,256,128]{2,3,1,0:T(8,128)}, u32[]{:S(2)}) copy-start(f32[2,3,256,128]{2,3,1,0:T(8,128)} %copy-done) | copy-start | bytes 2359300
  82.3 239.4 %all-gather.3.cloned.1.call-start = ((), (), s32[]{:S(2)}) async-start(), calls=%async_computation.6 | async-start | bytes 7077888 | tf_op jit(solution)/shard_map/all_gather | solution.py:128
  126.8 44.4 %copy-start.4 = (bf16[6144,96]{0,1:T(8,128)(2,1)S(1)}, bf16[6144,96]{0,1:T(8,128)(2,1)}, u32[]{:S(2)}) copy-start(bf16[6144,96]{0,1:T(8,128)(2,1)} %param.19) | copy-start | bytes 3538948
  130.4 22.5 %collective-permute-start = (bf16[128,1536]{0,1:T(8,128)(2,1)}, bf16[128,1536]{0,1:T(8,128)(2,1)S(1)}, u32[]{:S(2)}, u32[]{:S(2)}) collective-permute-start(bf16[128,1536]{0,1:T(8,128)(2,1)} %multiply_convert_fusion.2), channel_id=1, source_target_pairs={{0,2},{2,4},{4,6},{6,8},{8,10},{10,12},{12,14},{14,16},{16,18},{18... | collective-permute-start | bytes 1179656 | tf_op jit(solution)/shard_map/ppermute | solution.py:146
  152.9 15.6 %collective-permute-start.1 = (bf16[128,1536]{0,1:T(8,128)(2,1)S(1)}, bf16[128,1536]{0,1:T(8,128)(2,1)}, u32[]{:S(2)}, u32[]{:S(2)}) collective-permute-start(bf16[128,1536]{0,1:T(8,128)(2,1)S(1)} %collective-permute-done), channel_id=1, source_target_pairs={{0,2},{2,4},{4,6},{6,8},{8,10},{10,12},{12,14},{14,16},{16,18},{18... | collective-permute-start | bytes 1179656 | tf_op jit(solution)/shard_map/ppermute | solution.py:146
  152.9 23.8 %collective-permute-start.8 = (bf16[128,1536]{0,1:T(8,128)(2,1)}, bf16[128,1536]{0,1:T(8,128)(2,1)S(1)}, u32[]{:S(2)}, u32[]{:S(2)}) collective-permute-start(bf16[128,1536]{0,1:T(8,128)(2,1)} %multiply_convert_fusion.2), channel_id=1, source_target_pairs={{2,0},{4,2},{6,4},{8,6},{10,8},{12,10},{14,12},{16,14},{18,16},{20... | collective-permute-start | bytes 1179656 | tf_op jit(solution)/shard_map/ppermute | solution.py:148
  168.5 15.5 %collective-permute-start.2 = (bf16[128,1536]{0,1:T(8,128)(2,1)}, bf16[128,1536]{0,1:T(8,128)(2,1)}, u32[]{:S(2)}, u32[]{:S(2)}) collective-permute-start(bf16[128,1536]{0,1:T(8,128)(2,1)} %collective-permute-done.1), channel_id=1, source_target_pairs={{0,2},{2,4},{4,6},{6,8},{8,10},{10,12},{12,14},{14,16},{16,18},{18... | collective-permute-start | bytes 1179656 | tf_op jit(solution)/shard_map/ppermute | solution.py:146
  172.3 94.5 %all-to-all-start.1 = ((bf16[16,384,96]{1,2,0:T(8,128)(2,1)}), bf16[16,384,96]{1,2,0:T(8,128)(2,1)S(1)}, u32[]{:S(2)}, u32[]{:S(2)}) async-start(bf16[16,384,96]{1,2,0:T(8,128)(2,1)} %bitcast.89), calls=%async_computation.2 | async-start | bytes 2359296 | tf_op jit(solution)/shard_map/all_to_all | solution.py:129
  176.7 159.9 %all-gather.5.cloned.1.call-start = ((), (), s32[]{:S(2)}) async-start(), calls=%async_computation.7 | async-start | bytes 3538944 | tf_op jit(solution)/shard_map/all_gather | solution.py:130
  176.8 26.3 %collective-permute-start.9 = (bf16[128,1536]{0,1:T(8,128)(2,1)S(1)}, bf16[128,1536]{0,1:T(8,128)(2,1)S(1)}, u32[]{:S(2)}, u32[]{:S(2)}) collective-permute-start(bf16[128,1536]{0,1:T(8,128)(2,1)S(1)} %collective-permute-done.8), channel_id=1, source_target_pairs={{2,0},{4,2},{6,4},{8,6},{10,8},{12,10},{14,12},{16,14},{18,16},{20... | collective-permute-start | bytes 1179656 | tf_op jit(solution)/shard_map/ppermute | solution.py:148
  184.1 26.1 %collective-permute-start.3 = (bf16[128,1536]{0,1:T(8,128)(2,1)}, bf16[128,1536]{0,1:T(8,128)(2,1)S(1)}, u32[]{:S(2)}, u32[]{:S(2)}) collective-permute-start(bf16[128,1536]{0,1:T(8,128)(2,1)} %collective-permute-done.2), channel_id=1, source_target_pairs={{0,2},{2,4},{4,6},{6,8},{8,10},{10,12},{12,14},{14,16},{16,18},{18... | collective-permute-start | bytes 1179656 | tf_op jit(solution)/shard_map/ppermute | solution.py:146
  203.1 14.3 %collective-permute-start.10 = (bf16[128,1536]{0,1:T(8,128)(2,1)S(1)}, bf16[128,1536]{0,1:T(8,128)(2,1)S(1)}, u32[]{:S(2)}, u32[]{:S(2)}) collective-permute-start(bf16[128,1536]{0,1:T(8,128)(2,1)S(1)} %collective-permute-done.9), channel_id=1, source_target_pairs={{2,0},{4,2},{6,4},{8,6},{10,8},{12,10},{14,12},{16,14},{18,16},{20... | collective-permute-start | bytes 1179656 | tf_op jit(solution)/shard_map/ppermute | solution.py:148
  210.1 45.6 %copy-start.8 = (bf16[128,1536]{0,1:T(8,128)(2,1)}, bf16[128,1536]{0,1:T(8,128)(2,1)S(1)}, u32[]{:S(2)}) copy-start(bf16[128,1536]{0,1:T(8,128)(2,1)S(1)} %collective-permute-done.3) | copy-start | bytes 1179652
  210.2 17.7 %collective-permute-start.4 = (bf16[128,1536]{0,1:T(8,128)(2,1)S(1)}, bf16[128,1536]{0,1:T(8,128)(2,1)S(1)}, u32[]{:S(2)}, u32[]{:S(2)}) collective-permute-start(bf16[128,1536]{0,1:T(8,128)(2,1)S(1)} %collective-permute-done.3), channel_id=1, source_target_pairs={{0,2},{2,4},{4,6},{6,8},{8,10},{10,12},{12,14},{14,16},{16,18},{18... | collective-permute-start | bytes 1179656 | tf_op jit(solution)/shard_map/ppermute | solution.py:146
  217.3 19.1 %collective-permute-start.11 = (bf16[128,1536]{0,1:T(8,128)(2,1)S(1)}, bf16[128,1536]{0,1:T(8,128)(2,1)S(1)}, u32[]{:S(2)}, u32[]{:S(2)}) collective-permute-start(bf16[128,1536]{0,1:T(8,128)(2,1)S(1)} %collective-permute-done.10), channel_id=1, source_target_pairs={{2,0},{4,2},{6,4},{8,6},{10,8},{12,10},{14,12},{16,14},{18,16},{20... | collective-permute-start | bytes 1179656 | tf_op jit(solution)/shard_map/ppermute | solution.py:148
  227.8 38.8 %copy-start.9 = (bf16[128,1536]{0,1:T(8,128)(2,1)}, bf16[128,1536]{0,1:T(8,128)(2,1)S(1)}, u32[]{:S(2)}) copy-start(bf16[128,1536]{0,1:T(8,128)(2,1)S(1)} %collective-permute-done.4) | copy-start | bytes 1179652
  227.8 20.2 %collective-permute-start.5 = (bf16[128,1536]{0,1:T(8,128)(2,1)S(1)}, bf16[128,1536]{0,1:T(8,128)(2,1)S(1)}, u32[]{:S(2)}, u32[]{:S(2)}) collective-permute-start(bf16[128,1536]{0,1:T(8,128)(2,1)S(1)} %collective-permute-done.4), channel_id=1, source_target_pairs={{0,2},{2,4},{4,6},{6,8},{8,10},{10,12},{12,14},{14,16},{16,18},{18... | collective-permute-start | bytes 1179656 | tf_op jit(solution)/shard_map/ppermute | solution.py:146
  237.1 18.6 %collective-permute-start.12 = (bf16[128,1536]{0,1:T(8,128)(2,1)S(1)}, bf16[128,1536]{0,1:T(8,128)(2,1)}, u32[]{:S(2)}, u32[]{:S(2)}) collective-permute-start(bf16[128,1536]{0,1:T(8,128)(2,1)S(1)} %collective-permute-done.11), channel_id=1, source_target_pairs={{2,0},{4,2},{6,4},{8,6},{10,8},{12,10},{14,12},{16,14},{18,16},{20... | collective-permute-start | bytes 1179656 | tf_op jit(solution)/shard_map/ppermute | solution.py:148
  248.0 18.6 %copy-start.10 = (bf16[128,1536]{0,1:T(8,128)(2,1)}, bf16[128,1536]{0,1:T(8,128)(2,1)S(1)}, u32[]{:S(2)}) copy-start(bf16[128,1536]{0,1:T(8,128)(2,1)S(1)} %collective-permute-done.5) | copy-start | bytes 1179652
  248.0 18.6 %collective-permute-start.6 = (bf16[128,1536]{0,1:T(8,128)(2,1)S(1)}, bf16[128,1536]{0,1:T(8,128)(2,1)}, u32[]{:S(2)}, u32[]{:S(2)}) collective-permute-start(bf16[128,1536]{0,1:T(8,128)(2,1)S(1)} %collective-permute-done.5), channel_id=1, source_target_pairs={{0,2},{2,4},{4,6},{6,8},{8,10},{10,12},{12,14},{14,16},{16,18},{18... | collective-permute-start | bytes 1179656 | tf_op jit(solution)/shard_map/ppermute | solution.py:146
  255.7 18.0 %collective-permute-start.13 = (bf16[128,1536]{0,1:T(8,128)(2,1)}, bf16[128,1536]{0,1:T(8,128)(2,1)}, u32[]{:S(2)}, u32[]{:S(2)}) collective-permute-start(bf16[128,1536]{0,1:T(8,128)(2,1)} %collective-permute-done.12), channel_id=1, source_target_pairs={{2,0},{4,2},{6,4},{8,6},{10,8},{12,10},{14,12},{16,14},{18,16},{20... | collective-permute-start | bytes 1179656 | tf_op jit(solution)/shard_map/ppermute | solution.py:148
  266.7 18.1 %collective-permute-start.7 = (bf16[128,1536]{0,1:T(8,128)(2,1)}, bf16[128,1536]{0,1:T(8,128)(2,1)}, u32[]{:S(2)}, u32[]{:S(2)}) collective-permute-start(bf16[128,1536]{0,1:T(8,128)(2,1)} %collective-permute-done.6), channel_id=1, source_target_pairs={{0,2},{2,4},{4,6},{6,8},{8,10},{10,12},{12,14},{14,16},{16,18},{18... | collective-permute-start | bytes 1179656 | tf_op jit(solution)/shard_map/ppermute | solution.py:146
  267.9 33.3 %copy-start.7 = (bf16[128,1536]{0,1:T(8,128)(2,1)S(1)}, bf16[128,1536]{0,1:T(8,128)(2,1)}, u32[]{:S(2)}) copy-start(bf16[128,1536]{0,1:T(8,128)(2,1)} %copy-done.6) | copy-start | bytes 1179652
  267.9 227.3 %reduce-scatter.8.cloned.1.call-start = ((), (), s32[]{:S(2)}) async-start(), calls=%async_computation.8 | async-start | bytes 6684672 | tf_op jit(solution)/shard_map/reduce_scatter | solution.py:157
  273.8 31.7 %collective-permute-start.14 = (bf16[128,1536]{0,1:T(8,128)(2,1)}, bf16[128,1536]{0,1:T(8,128)(2,1)S(1)}, u32[]{:S(2)}, u32[]{:S(2)}) collective-permute-start(bf16[128,1536]{0,1:T(8,128)(2,1)} %collective-permute-done.13), channel_id=1, source_target_pairs={{2,0},{4,2},{6,4},{8,6},{10,8},{12,10},{14,12},{16,14},{18,16},{20... | collective-permute-start | bytes 1179656 | tf_op jit(solution)/shard_map/ppermute | solution.py:148
  (6 other events, 34.7 us)
Sparse Core Ops, SparseCore 0:
  45.1 10.0 reduce-scatter.9
  82.4 10.3 reduce-scatter.5
  126.9 24.3 all-gather.2
  268.0 13.2 all-gather.4
  345.9 149.2 reduce-scatter.7
